TPU v7x, 512 devices: a whole 4x4x16 slice. The times are simulated.
512 devices in a mesh: dp: 8 (over y, core), row: 64 (over x, z).
Axes of the slice: x: 4, y: 4, z: 16, core: 2. Of those that a mesh axis runs over, the one named last changes fastest.
Arguments:
- hidden: bfloat16 [8, 128, 128, 768], P('dp', 'row'), may hold values from -6 to 6
- masked: int32 [8, 128, 128], P('dp', 'row'), may hold values 0 or 1
- depths: int32 [8], P('dp'), may hold values from 32 to 128, as said below
- norm_gain: float32 [768], replicated, may hold values from 0.25 to 1.75
- w_query: bfloat16 [768, 768], P('row'), may hold values from -0.21875 to 0.21875
- w_key: bfloat16 [768, 768], P('row'), may hold values from -0.21875 to 0.21875
- w_value: bfloat16 [768, 768], P('row'), may hold values from -0.21875 to 0.21875
- w_out: bfloat16 [768, 768], P('row'), may hold values from -0.21875 to 0.21875
- cotangent: bfloat16 [8, 128, 128, 768], P('dp', 'row'), may hold values from -6 to 6
Outputs:
- mixed: bfloat16 [8, 128, 128, 768], P('dp', 'row')
- grad_hidden: bfloat16 [8, 128, 128, 768], P('dp', 'row')
Inputs may be any that keep to these rules, and one draw needn't show every extreme that they name: `depths`: rows at or past an MSA's depth are padding.
All inputs are finite; a program needn't handle non-finite values. No bound on the sum of `masked` on one device may be relied on, other than what follows from the above.
Results may differ from a plain program's by a relative error of at most 0.0059.
Values may be sent and summed in bfloat16 or wider, within the bound.
A program may use at most 64 MiB of HBM per device.

v0:
```python
import jax
import jax.numpy as jnp
from jax import lax
from jax.sharding import PartitionSpec as P

HEADS = 12
EPS = 1e-05


def softmax_rows(scores):
    top = jnp.max(scores, axis=-1, keepdims=True)
    expo = jnp.exp(scores - top)
    return expo / jnp.sum(expo, axis=-1, keepdims=True)


def back_dot(left, weight):
    return lax.dot_general(
        left, weight, (((1,), (1,)), ((), ())), preferred_element_type=jnp.float32
    )


def body(hidden, masked, depths, norm_gain, w_query, w_key, w_value, w_out, cotangent):
    local_rows = hidden.shape[1]
    columns = hidden.shape[2]
    width = hidden.shape[3]
    head_count = HEADS
    head_size = width // head_count
    flat_rows = local_rows * columns
    first_row = lax.axis_index("row") * local_rows
    depth = depths[0]
    alive = (first_row + jnp.arange(local_rows, dtype=jnp.int32) < depth).astype(jnp.float32)
    mask_rows = masked[0]
    weighting = mask_rows.astype(jnp.float32) * alive[:, None]
    live_total, masked_total = lax.psum(
        (jnp.sum(alive) * columns, jnp.sum(weighting)), ("dp", "row")
    )
    loss_ratio = live_total / jnp.maximum(masked_total, 1.0)
    full_query, full_key, full_value, full_out = (
        lax.all_gather(w_query, "row", axis=0, tiled=True),
        lax.all_gather(w_key, "row", axis=0, tiled=True),
        lax.all_gather(w_value, "row", axis=0, tiled=True),
        lax.all_gather(w_out, "row", axis=0, tiled=True),
    )
    widened = hidden[0].reshape(flat_rows, width).astype(jnp.float32)
    average = jnp.mean(widened, axis=-1, keepdims=True)
    centred = widened - average
    variance = jnp.mean(centred * centred, axis=-1, keepdims=True)
    inv_std = lax.rsqrt(variance + EPS)
    x_hat = centred * inv_std
    normed = (x_hat * norm_gain).astype(jnp.bfloat16)

    def project(weight):
        out = jnp.dot(normed, weight, preferred_element_type=jnp.float32).astype(jnp.bfloat16)
        return out.reshape(local_rows, columns, head_count, head_size)

    queries = project(full_query)
    keys_proj = project(full_key)
    values_proj = project(full_value)
    alive_heads = alive[:, None, None, None]
    query_live = queries * alive_heads.astype(jnp.bfloat16)
    scale = 1.0 / jnp.sqrt(depth.astype(jnp.float32) * head_size)
    partial_value = jnp.einsum(
        "rihe,rjhe->hij", query_live, keys_proj, preferred_element_type=jnp.float32
    )
    logits = lax.psum(partial_value, "row") * scale
    probs = softmax_rows(logits)
    probs_low = probs.astype(jnp.bfloat16)
    attended = jnp.einsum(
        "hij,rjhe->rihe", probs_low, values_proj, preferred_element_type=jnp.float32
    ).astype(jnp.bfloat16)
    projected = jnp.dot(
        attended.reshape(flat_rows, width), full_out, preferred_element_type=jnp.float32
    )
    alive_tokens = jnp.repeat(alive, columns)[:, None]
    mixed = (widened + alive_tokens * projected).astype(jnp.bfloat16)
    back_query, back_key, back_value, back_out = (
        lax.all_gather(w_query, "row", axis=0, tiled=True),
        lax.all_gather(w_key, "row", axis=0, tiled=True),
        lax.all_gather(w_value, "row", axis=0, tiled=True),
        lax.all_gather(w_out, "row", axis=0, tiled=True),
    )
    token_weight = (weighting * loss_ratio).reshape(flat_rows, 1)
    grad_mixed = cotangent[0].reshape(flat_rows, width).astype(jnp.float32) * token_weight
    grad_attended = back_dot(grad_mixed.astype(jnp.bfloat16), back_out).astype(jnp.bfloat16)
    grad_attended = grad_attended.reshape(local_rows, columns, head_count, head_size)
    grad_partial = jnp.einsum(
        "rihe,rjhe->hij", grad_attended, values_proj, preferred_element_type=jnp.float32
    )
    grad_values = jnp.einsum(
        "hij,rihe->rjhe", probs_low, grad_attended, preferred_element_type=jnp.float32
    ).astype(jnp.bfloat16)
    grad_probs = lax.psum(grad_partial, "row")
    grad_logits = probs * (grad_probs - jnp.sum(probs * grad_probs, axis=-1, keepdims=True))
    grad_logits = (grad_logits * scale).astype(jnp.bfloat16)
    grad_queries = (
        jnp.einsum("hij,rjhe->rihe", grad_logits, keys_proj, preferred_element_type=jnp.float32)
        * alive_heads
    ).astype(jnp.bfloat16)
    grad_keys = jnp.einsum(
        "hij,rihe->rjhe", grad_logits, query_live, preferred_element_type=jnp.float32
    ).astype(jnp.bfloat16)
    grad_normed = back_dot(grad_queries.reshape(flat_rows, width), back_query)
    grad_normed = grad_normed + back_dot(grad_keys.reshape(flat_rows, width), back_key)
    grad_normed = grad_normed + back_dot(grad_values.reshape(flat_rows, width), back_value)
    scaled = grad_normed * norm_gain
    grad_x = inv_std * (
        scaled
        - jnp.mean(scaled, axis=-1, keepdims=True)
        - x_hat * jnp.mean(scaled * x_hat, axis=-1, keepdims=True)
    )
    grad_hidden = (grad_mixed + grad_x).astype(jnp.bfloat16)
    return (
        mixed.reshape(1, local_rows, columns, width),
        grad_hidden.reshape(1, local_rows, columns, width),
    )


def solution(mesh):
    return jax.shard_map(
        body,
        mesh=mesh,
        in_specs=(
            P("dp", "row", None, None),
            P("dp", "row", None),
            P("dp"),
            P(),
            P("row", None),
            P("row", None),
            P("row", None),
            P("row", None),
            P("dp", "row", None, None),
        ),
        out_specs=(P("dp", "row", None, None), P("dp", "row", None, None)),
        check_vma=False,
    )
```

profile of v0, /device:TPU:8, one launch (start us, length us, event | category | flops | bytes accessed | tf_op | source)
XLA Modules:
  0.0 913.6 jit_solution(1743458833186725922)
XLA Ops:
  7.2 0.7 all-gather.13.cloned.1.call-update
  8.0 0.7 all-gather.9.cloned.1.call-update
  8.7 0.7 all-gather.11.cloned.1.call-update
  9.4 0.5 all-gather.15.cloned.1.call-update
  10.7 0.6 fusion.67
  11.9 1.9 broadcast_bitcast_fusion
  13.9 108.7 %all-reduce = (f32[]{:T(128)}, f32[]{:T(128)}) all-reduce(f32[]{:T(128)S(6)} %mul.140, f32[]{:T(128)} %get-tuple-element.13), channel_id=1, replica_groups=mesh['dp'=8,'row'=64] {'dp','row'}, use_global_device_ids=true, to_apply=%region_6.0 | all-reduce | flops 2 | bytes 16 | tf_op jit(solution)/shard_map/psum | solution.py:34
  123.9 1.1 convert_reduce_fusion
  125.0 1.2 multiply_reduce_fusion.1
  126.3 0.8 fusion.54
  127.1 0.9 multiply_convert_fusion
  128.0 28.0 %all-gather.13.cloned.1.call-done = bf16[64,12,768]{2,1,0:T(8,128)(2,1)} async-done(((bf16[1,12,768]{2,1,0:T(8,128)(2,1)}), bf16[64,12,768]{2,1,0:T(8,128)(2,1)}) %all-gather.13.cloned.1.call-update) | async-done | bytes 1179664 | tf_op jit(solution)/shard_map/all_gather | solution.py:40
  155.9 2.2 reshape.134
  158.2 0.5 convolution_convert_fusion.1
  158.9 0.8 reshape.119
  159.7 135.6 %all-gather.9.cloned.1.call-done = bf16[64,12,768]{2,1,0:T(8,128)(2,1)} async-done(((bf16[1,12,768]{2,1,0:T(8,128)(2,1)}), bf16[64,12,768]{2,1,0:T(8,128)(2,1)}) %all-gather.9.cloned.1.call-update) | async-done | bytes 1179664 | tf_op jit(solution)/shard_map/all_gather | solution.py:41
  295.3 2.2 reshape.130
  297.6 0.5 convolution_convert_fusion.3
  298.2 0.8 reshape.117
  299.1 135.7 %all-gather.11.cloned.1.call-done = bf16[64,12,768]{2,1,0:T(8,128)(2,1)} async-done(((bf16[1,12,768]{2,1,0:T(8,128)(2,1)}), bf16[64,12,768]{2,1,0:T(8,128)(2,1)}) %all-gather.11.cloned.1.call-update) | async-done | bytes 1179664 | tf_op jit(solution)/shard_map/all_gather | solution.py:39
  434.7 2.2 reshape.132
  437.0 2.2 convolution_convert_fusion.2
  439.2 1.9 copy.35
  441.1 1.8 reshape.118
  443.0 131.0 %all-gather.15.cloned.1.call-done = bf16[64,12,768]{2,1,0:T(8,128)(2,1)} async-done(((bf16[1,12,768]{2,1,0:T(8,128)(2,1)}), bf16[64,12,768]{2,1,0:T(8,128)(2,1)}) %all-gather.15.cloned.1.call-update) | async-done | bytes 1179664 | tf_op jit(solution)/shard_map/all_gather | solution.py:42
  574.0 3.1 reshape.136
  577.1 2.7 convolution_convert_fusion
  579.8 1.9 copy.41
  581.7 1.8 reshape.122
  583.5 1.4 broadcast_multiply_fusion
  585.0 2.5 convolution_bitcast_fusion
  587.5 1.2 convolution_bitcast_fusion.1
  588.8 275.2 %all-reduce.4.cloned.1.call-done = (f32[12,128,128]{2,1,0:T(8,128)}, f32[12,128,128]{2,1,0:T(8,128)}) async-done(((f32[12,128,128]{2,1,0:T(8,128)}, f32[12,128,128]{2,1,0:T(8,128)}), (f32[12,128,128]{2,1,0:T(8,128)}, f32[12,128,128]{2,1,0:T(8,128)})) %all-reduce.4.cloned.1.call-update) | async-done | bytes 1572880 | tf_op jit(solution)/shard_map/psum | solution.py:65
  864.0 2.3 fusion.68
  866.3 10.9 %fusion.15 = bf16[2,128,12,64]{1,3,0,2:T(8,128)(2,1)} fusion(f32[12,128,128]{2,1,0:T(8,128)} %get-tuple-element.7, f32[2]{0:T(128)} %copy-done.10, f32[]{:T(128)S(6)} %sqrt.3, bf16[2,128,12,64]{1,0,3,2:T(2,128)(2,1)} %reshape.119, f32[12,128,128]{2,1,0:T(8,128)} %get-tuple-element.15, f32[12,128]{1,0:T(8,128)S(1)} %get-tuple-element.14), kind=kOutput, calls=%fused_computation.28 | convolution fusion | flops 52102784 | bytes 2365452 | tf_op jit(solution)/shard_map/hij,rjhe->rihe/dot_general | solution.py:96
  877.2 10.9 %fusion.13 = bf16[2,128,12,64]{1,3,0,2:T(8,128)(2,1)} fusion(f32[12,128,128]{2,1,0:T(8,128)} %get-tuple-element.7, f32[]{:T(128)S(6)} %sqrt.3, bf16[2,128,12,64]{1,0,3,2:T(2,128)(2,1)} %copy-done.4, f32[12,128,128]{2,1,0:T(8,128)} %get-tuple-element.15, f32[12,128]{1,0:T(8,128)S(1)} %get-tuple-element.14), kind=kOutput, calls=%fused_computation.26 | convolution fusion | flops 51906176 | bytes 2365444 | tf_op jit(solution)/shard_map/hij,rihe->rjhe/dot_general | solution.py:99
  888.1 4.8 fusion.14
  892.9 4.8 fusion.12
  897.7 1.4 copy.47
  899.1 1.4 copy.45
  900.6 0.5 fusion.32
  901.1 0.5 copy-done.8
  902.4 0.5 convolution_add_fusion.1
  902.9 0.4 copy-done.1
  903.4 0.7 fusion.66
  904.1 0.5 copy-done.5
  904.7 1.3 fusion.9
  905.9 1.1 fusion.19
  (39 shorter events, 1.4 us)
Async XLA Ops:
  7.2 119.9 %copy-start = (bf16[1,2,128,768]{3,2,1,0:T(8,128)(2,1)S(1)}, bf16[1,2,128,768]{3,2,1,0:T(8,128)(2,1)}, u32[]{:S(2)}) copy-start(bf16[1,2,128,768]{3,2,1,0:T(8,128)(2,1)} %param.9) | copy-start | bytes 1179652
  7.2 148.8 %all-gather.13.cloned.1.call-start = ((), (), s32[]{:S(2)}) async-start(), calls=%async_computation.2 | async-start | bytes 1597440 | tf_op jit(solution)/shard_map/all_gather | solution.py:40
  7.9 287.4 %all-gather.9.cloned.1.call-start = ((), (), s32[]{:S(2)}) async-start(), calls=%async_computation | async-start | bytes 1597440 | tf_op jit(solution)/shard_map/all_gather | solution.py:41
  8.7 426.1 %all-gather.11.cloned.1.call-start = ((), (), s32[]{:S(2)}) async-start(), calls=%async_computation.1 | async-start | bytes 1597440 | tf_op jit(solution)/shard_map/all_gather | solution.py:39
  9.4 564.6 %all-gather.15.cloned.1.call-start = ((), (), s32[]{:S(2)}) async-start(), calls=%async_computation.3 | async-start | bytes 1597440 | tf_op jit(solution)/shard_map/all_gather | solution.py:42
  10.0 854.0 %all-reduce.4.cloned.1.call-start = ((), (), s32[]{:S(2)}) async-start(), calls=%async_computation.4 | async-start | bytes 3145728 | tf_op jit(solution)/shard_map/psum | solution.py:65
  11.3 116.7 %copy-start.10 = (f32[2]{0:T(128)}, f32[2]{0:T(128)S(1)}, u32[]{:S(2)}) copy-start(f32[2]{0:T(128)S(1)} %get-tuple-element.9) | copy-start | bytes 28
  127.0 450.1 %copy-start.11 = (f32[256]{0:T(256)}, f32[256]{0:T(256)S(1)}, u32[]{:S(2)}) copy-start(f32[256]{0:T(256)S(1)} %fusion.54) | copy-start | bytes 3076
  128.0 169.6 %copy-start.2 = (bf16[256,768]{1,0:T(8,128)(2,1)}, bf16[256,768]{1,0:T(8,128)(2,1)S(1)}, u32[]{:S(2)}) copy-start(bf16[256,768]{1,0:T(8,128)(2,1)S(1)} %multiply_convert_fusion) | copy-start | bytes 1179652
  583.5 3.9 copy-start.3
  585.0 2.5 copy-start.4
  900.6 1.0 copy-start.8
  900.6 1.4 copy-start.7
  902.4 1.0 copy-start.1
  902.4 1.0 copy-start.9
  903.4 1.3 copy-start.5
  903.4 1.3 copy-start.13
  904.7 1.3 copy-start.6
  904.7 1.3 copy-start.12
Sparse Core Ops, SparseCore 0:
  10.9 144.9 all-gather.12
  158.9 136.3 all-gather.8
  298.2 136.4 all-gather.10
  437.5 136.4 all-gather.14
  588.8 275.0 all-reduce.3
where the time goes:
time: 915 us; the launch traced here: 914 us
  waiting for transfers between devices  708 us (77%)
  blocking collectives  109 us (12%)
  matrix products  44 us (5%)
  local copies, waits for them, and re-layouts  24.6 us (3%)
  between operations  16.6 us (2%)
  other arithmetic  11.4 us (1%)
    psum x1, waiting for transfers between devices, body(): logits = lax.psum(partial_value, 'row') * scale  275 us
    all_gather x1, waiting for transfers between devices, body(): lax.all_gather(w_query, 'row', axis=0, tiled=True)  136 us
    all_gather x1, waiting for transfers between devices, body(): lax.all_gather(w_value, 'row', axis=0, tiled=True)  136 us
    all_gather x1, waiting for transfers between devices, body(): lax.all_gather(w_out, 'row', axis=0, tiled=True)  131 us
    psum x1, blocking collectives, body(): lax.psum((jnp.sum(alive) * columns, jnp.sum(weighting)), ('dp', 'row'))  109 us
    all_gather x1, waiting for transfers between devices, body(): lax.all_gather(w_key, 'row', axis=0, tiled=True)  28 us
  transfers between devices with their start and end apart: 5, of which 5 were waited for; matrix products, arithmetic and copies ran while one was open for 2% of the time, Pallas kernels for 0%

commit v1 on v0

--- a/solution.py
+++ b/solution.py
@@ -39,7 +39,9 @@
         lax.all_gather(w_query, "row", axis=0, tiled=True),
         lax.all_gather(w_key, "row", axis=0, tiled=True),
         lax.all_gather(w_value, "row", axis=0, tiled=True),
-        lax.all_gather(w_out, "row", axis=0, tiled=True),
+        jnp.concatenate(
+            lax.all_to_all(jnp.stack([w_out] * lax.axis_size("row")), "row", 0, 0), axis=0
+        ),
     )
     widened = hidden[0].reshape(flat_rows, width).astype(jnp.float32)
     average = jnp.mean(widened, axis=-1, keepdims=True)

time: 915 us -> 937 us (1.024)
  waiting for transfers between devices: 708 us -> 671 us
  blocking collectives: 109 us -> 139 us
  starting transfers between devices: 0.19 us -> 19.1 us
  local copies, waits for them, and re-layouts: 24.6 us -> 35.2 us
    all_gather x1, waiting for transfers between devices: 136 us -> 0.02 us  [body(): lax.all_gather(w_query, 'row', axis=0, tiled=True)]
    all_gather x1, waiting for transfers between devices: 28 us -> 122 us  [body(): lax.all_gather(w_key, 'row', axis=0, tiled=True)]
    psum x1, blocking collectives: 109 us -> 139 us  [body(): lax.psum((jnp.sum(alive) * columns, jnp.sum(weighting)), ('dp', 'row'))]
    all_to_all x0 -> x1, starting transfers between devices: none -> 18.9 us  [body(): lax.all_to_all(jnp.stack([w_out] * lax.axis_size('row')), 'row', 0, 0)]
  transfers between devices with their start and end apart: 5 -> 6, of which waited for: 5 -> 4; matrix products, arithmetic and copies ran while one was open for 2% -> 9% of each run, Pallas kernels for 0% -> 0%
where the time goes in v1:
time: 937 us; the launch traced here: 936 us
  waiting for transfers between devices  671 us (72%)
  blocking collectives  139 us (15%)
  matrix products  45.9 us (5%)
  local copies, waits for them, and re-layouts  35.2 us (4%)
  starting transfers between devices  19.1 us (2%)
  between operations  16.6 us (2%)
    psum x1, waiting for transfers between devices, body(): logits = lax.psum(partial_value, 'row') * scale  275 us
    psum x1, blocking collectives, body(): lax.psum((jnp.sum(alive) * columns, jnp.sum(weighting)), ('dp', 'row'))  139 us
    all_gather x1, waiting for transfers between devices, body(): lax.all_gather(w_value, 'row', axis=0, tiled=True)  137 us
    all_gather x1, waiting for transfers between devices, body(): lax.all_gather(w_out, 'row', axis=0, tiled=True)  133 us
    all_gather x1, waiting for transfers between devices, body(): lax.all_gather(w_key, 'row', axis=0, tiled=True)  122 us
    all_to_all x1, starting transfers between devices, body(): lax.all_to_all(jnp.stack([w_out] * lax.axis_size('row')), 'row', 0, 0)  18.9 us
  transfers between devices with their start and end apart: 6, of which 4 were waited for; matrix products, arithmetic and copies ran while one was open for 9% of the time, Pallas kernels for 0%

profile of v1, /device:TPU:8, one launch (start us, length us, event | category | flops | bytes accessed | tf_op | source)
XLA Modules:
  0.0 936.2 jit_solution(6862891457699644232)
XLA Ops:
  7.2 0.7 all-gather.11.cloned.1.call-update
  7.9 0.7 all-gather.13.cloned.1.call-update
  8.7 0.7 all-gather.9.cloned.1.call-update
  9.4 2.0 stack.2
  11.4 18.9 %all-to-all-start = ((bf16[64,12,768]{2,1,0:T(8,128)(2,1)}), bf16[64,12,768]{2,1,0:T(8,128)(2,1)}, u32[]{:S(2)}, u32[]{:S(2)}) async-start(bf16[64,12,768]{2,1,0:T(8,128)(2,1)} %stack.2), calls=%async_computation | async-start | bytes 3145728 | tf_op jit(solution)/shard_map/all_to_all | solution.py:43
  30.4 0.5 all-gather.15.cloned.1.call-update
  31.6 0.6 fusion.67
  32.8 1.3 broadcast_bitcast_fusion
  34.1 139.5 %all-reduce = (f32[]{:T(128)}, f32[]{:T(128)}) all-reduce(f32[]{:T(128)S(6)} %mul.140, f32[]{:T(128)} %get-tuple-element.13), channel_id=1, replica_groups=mesh['dp'=8,'row'=64] {'dp','row'}, use_global_device_ids=true, to_apply=%region_6.0 | all-reduce | flops 2 | bytes 16 | tf_op jit(solution)/shard_map/psum | solution.py:34
  173.6 0.6 convert_element_type.115
  175.9 0.7 fusion.54
  176.8 2.4 reshape.138
  179.2 0.5 convolution_convert_fusion.2
  179.9 0.9 reshape.123
  180.7 122.4 %all-gather.13.cloned.1.call-done = bf16[64,12,768]{2,1,0:T(8,128)(2,1)} async-done(((bf16[1,12,768]{2,1,0:T(8,128)(2,1)}), bf16[64,12,768]{2,1,0:T(8,128)(2,1)}) %all-gather.13.cloned.1.call-update) | async-done | bytes 1179664 | tf_op jit(solution)/shard_map/all_gather | solution.py:40
  303.2 2.2 reshape.140
  305.4 137.2 %all-gather.9.cloned.1.call-done = bf16[64,12,768]{2,1,0:T(8,128)(2,1)} async-done(((bf16[1,12,768]{2,1,0:T(8,128)(2,1)}), bf16[64,12,768]{2,1,0:T(8,128)(2,1)}) %all-gather.9.cloned.1.call-update) | async-done | bytes 1179664 | tf_op jit(solution)/shard_map/all_gather | solution.py:41
  442.6 2.2 reshape.136
  444.8 2.3 convolution_convert_fusion.1
  447.1 1.2 convolution_convert_fusion.3
  448.4 133.5 %all-gather.15.cloned.1.call-done = bf16[64,12,768]{2,1,0:T(8,128)(2,1)} async-done(((bf16[1,12,768]{2,1,0:T(8,128)(2,1)}), bf16[64,12,768]{2,1,0:T(8,128)(2,1)}) %all-gather.15.cloned.1.call-update) | async-done | bytes 1179664 | tf_op jit(solution)/shard_map/all_gather | solution.py:82
  581.9 3.1 reshape.142
  585.0 2.7 convolution_convert_fusion
  587.7 1.2 broadcast_multiply_fusion
  588.9 1.9 copy.41
  590.8 1.9 reshape.128
  592.6 1.9 copy.36
  594.5 1.8 reshape.124
  596.4 1.9 copy.34
  598.3 1.8 reshape.122
  600.1 2.4 convolution_bitcast_fusion.1
  602.5 1.3 convolution_bitcast_fusion
  603.9 275.3 %all-reduce.4.cloned.1.call-done = (f32[12,128,128]{2,1,0:T(8,128)}, f32[12,128,128]{2,1,0:T(8,128)}) async-done(((f32[12,128,128]{2,1,0:T(8,128)}, f32[12,128,128]{2,1,0:T(8,128)}), (f32[12,128,128]{2,1,0:T(8,128)}, f32[12,128,128]{2,1,0:T(8,128)})) %all-reduce.4.cloned.1.call-update) | async-done | bytes 1572880 | tf_op jit(solution)/shard_map/psum | solution.py:67
  879.1 2.9 fusion.68
  882.0 11.0 %fusion.13 = bf16[2,128,12,64]{1,3,0,2:T(8,128)(2,1)} fusion(f32[12,128,128]{2,1,0:T(8,128)} %get-tuple-element.7, f32[]{:T(128)S(6)} %sqrt.3, bf16[2,128,12,64]{1,0,3,2:T(2,128)(2,1)} %broadcast_multiply_fusion, f32[12,128,128]{2,1,0:T(8,128)} %get-tuple-element.15, f32[12,128]{1,0:T(8,128)} %get-tuple-element.14), kind=kOutput, calls=%fused_computation.26 | convolution fusion | flops 51906176 | bytes 2365444 | tf_op jit(solution)/shard_map/hij,rihe->rjhe/dot_general | solution.py:101
  893.0 2.2 copy.47
  895.2 10.9 %fusion.15 = bf16[2,128,12,64]{1,3,0,2:T(8,128)(2,1)} fusion(f32[12,128,128]{2,1,0:T(8,128)} %get-tuple-element.7, f32[2]{0:T(128)S(1)} %get-tuple-element.9, f32[]{:T(128)S(6)} %sqrt.3, bf16[2,128,12,64]{1,0,3,2:T(2,128)(2,1)} %reshape.124, f32[12,128,128]{2,1,0:T(8,128)} %get-tuple-element.15, f32[12,128]{1,0:T(8,128)} %get-tuple-element.14), kind=kOutput, calls=%fused_computation.28 | convolution fusion | flops 52102784 | bytes 2365452 | tf_op jit(solution)/shard_map/hij,rjhe->rihe/dot_general | solution.py:98
  906.1 2.1 copy.45
  908.3 4.8 fusion.12
  913.1 2.1 copy.40
  915.2 4.8 fusion.14
  920.0 1.4 copy.49
  921.4 1.6 fusion.32
  923.0 0.5 convolution_add_fusion.1
  924.0 0.7 fusion.66
  925.0 1.1 fusion.19
  926.1 2.3 reshape.126
  928.4 1.3 fusion.9
  (45 shorter events, 1.8 us)
Async XLA Ops:
  7.2 169.7 %all-gather.11.cloned.1.call-start = ((), (), s32[]{:S(2)}) async-start(), calls=%async_computation.2 | async-start | bytes 1597440 | tf_op jit(solution)/shard_map/all_gather | solution.py:39
  7.9 295.3 %all-gather.13.cloned.1.call-start = ((), (), s32[]{:S(2)}) async-start(), calls=%async_computation.3 | async-start | bytes 1597440 | tf_op jit(solution)/shard_map/all_gather | solution.py:40
  8.6 433.9 %all-gather.9.cloned.1.call-start = ((), (), s32[]{:S(2)}) async-start(), calls=%async_computation.1 | async-start | bytes 1597440 | tf_op jit(solution)/shard_map/all_gather | solution.py:41
  11.4 21.5 %copy-start.12 = (s32[1,2,128]{2,1,0:T(2,128)S(1)}, s32[1,2,128]{2,1,0:T(2,128)}, u32[]{:S(2)}) copy-start(s32[1,2,128]{2,1,0:T(2,128)} %param.10) | copy-start | bytes 3076
  11.4 164.1 %copy-start = (bf16[1,2,128,768]{3,2,1,0:T(8,128)(2,1)S(1)}, bf16[1,2,128,768]{3,2,1,0:T(8,128)(2,1)}, u32[]{:S(2)}) copy-start(bf16[1,2,128,768]{3,2,1,0:T(8,128)(2,1)} %param.9) | copy-start | bytes 1179652
  11.4 165.2 %copy-start.10 = (f32[768]{0:T(1024)S(1)}, f32[768]{0:T(1024)}, u32[]{:S(2)}) copy-start(f32[768]{0:T(1024)} %param.12) | copy-start | bytes 9220
  11.4 914.7 %all-to-all-start = ((bf16[64,12,768]{2,1,0:T(8,128)(2,1)}), bf16[64,12,768]{2,1,0:T(8,128)(2,1)}, u32[]{:S(2)}, u32[]{:S(2)}) async-start(bf16[64,12,768]{2,1,0:T(8,128)(2,1)} %stack.2), calls=%async_computation | async-start | bytes 3145728 | tf_op jit(solution)/shard_map/all_to_all | solution.py:43
  30.3 551.6 %all-gather.15.cloned.1.call-start = ((), (), s32[]{:S(2)}) async-start(), calls=%async_computation.4 | async-start | bytes 1597440 | tf_op jit(solution)/shard_map/all_gather | solution.py:82
  30.9 848.3 %all-reduce.4.cloned.1.call-start = ((), (), s32[]{:S(2)}) async-start(), calls=%async_computation.5 | async-start | bytes 3145728 | tf_op jit(solution)/shard_map/psum | solution.py:67
  176.8 2.4 copy-start.2
  444.8 2.3 copy-start.3
  585.0 2.7 copy-start.7
  585.0 2.7 copy-start.14
  600.1 2.4 copy-start.5
  600.1 2.4 copy-start.6
  921.4 1.6 copy-start.4
  923.0 1.0 copy-start.1
  924.0 1.0 copy-start.8
  924.0 1.0 copy-start.11
  926.1 2.3 copy-start.9
  926.1 2.3 copy-start.13
Sparse Core Ops, SparseCore 0:
  10.9 152.7 all-gather.10
  166.7 136.4 all-gather.12
  306.1 136.4 all-gather.8
  445.4 136.4 all-gather.14
  603.9 275.1 all-reduce.3
